TPU v7x, 32 devices: a whole 2x2x4 slice. The times are simulated.
32 devices in a mesh: row: 4 (over y, core), col: 4 (over z), exp: 2 (over x).
Axes of the slice: x: 2, y: 2, z: 4, core: 2. Of those that a mesh axis runs over, the one named last changes fastest.
Arguments:
- tokens: bfloat16 [4096, 2048], P(('row', 'exp')), may hold values from -6 to 6
- attn_gain: bfloat16 [2048], P(('row', 'exp')), may hold values from 0.5 to 1.5
- query_proj: bfloat16 [2048, 3072], P(('row', 'exp'), 'col'), may hold values from -0.125 to 0.125
- latent_proj: bfloat16 [2048, 576], P(('row', 'exp'), 'col'), may hold values from -0.125 to 0.125
- latent_gain: bfloat16 [512], P(('row', 'exp')), may hold values from 0.5 to 1.5
- keyval_proj: bfloat16 [512, 4096], P(('row', 'exp'), 'col'), may hold values from -0.25 to 0.25
- output_proj: bfloat16 [2048, 2048], P('col', ('row', 'exp')), may hold values from -0.5 to 0.5
- mixer_gain: bfloat16 [2048], P(('row', 'exp')), may hold values from 0.5 to 1.5
- router_proj: bfloat16 [2048, 16], P(('row', 'exp')), may hold values from -0.046875 to 0.046875
- shared_gate: bfloat16 [2048, 2816], P(('row', 'exp'), 'col'), may hold values from -0.125 to 0.125
- shared_up: bfloat16 [2048, 2816], P(('row', 'exp'), 'col'), may hold values from -0.125 to 0.125
- shared_down: bfloat16 [2816, 2048], P('col', ('row', 'exp')), may hold values from -0.109375 to 0.109375
- expert_gate: bfloat16 [16, 2048, 1408], P(('row', 'exp'), None, 'col'), may hold values from -0.125 to 0.125
- expert_up: bfloat16 [16, 2048, 1408], P(('row', 'exp'), None, 'col'), may hold values from -0.125 to 0.125
- expert_down: bfloat16 [16, 1408, 2048], P(('row', 'exp'), 'col'), may hold values from -0.25 to 0.25
- routes: int32 [4096, 6], P(('row', 'exp')), may hold values from 0 to 15, all different within a row; in each aligned block of 512 rows (0 to 511, 512 to 1023, ...) at most 274 rows name the same one
- segments: int32 [8, 512], P(('row', 'exp')), may hold values from 0 to 1, never falling along the last dimension, each value on 1 to 384 neighbouring positions
- cotangent: bfloat16 [4096, 2048], P(('row', 'exp')), may hold values from -6 to 6
Outputs:
- layer_out: bfloat16 [4096, 2048], P(('row', 'exp'), 'col')
- tokens_grad: float32 [4096, 2048], P(('row', 'exp'))
- attn_gain_grad: float32 [2048], P(('row', 'exp'))
- query_grad: float32 [2048, 3072], P(('row', 'exp'), 'col')
- latent_grad: float32 [2048, 576], P(('row', 'exp'), 'col')
- latent_gain_grad: float32 [512], P(('row', 'exp'))
- keyval_grad: float32 [512, 4096], P(('row', 'exp'), 'col')
- output_grad: float32 [2048, 2048], P('col', ('row', 'exp'))
- mixer_gain_grad: float32 [2048], P(('row', 'exp'))
- router_grad: float32 [2048, 16], P(('row', 'exp'))
- shared_gate_grad: float32 [2048, 2816], P(('row', 'exp'), 'col')
- shared_up_grad: float32 [2048, 2816], P(('row', 'exp'), 'col')
- shared_down_grad: float32 [2816, 2048], P('col', ('row', 'exp'))
- expert_gate_grad: float32 [16, 2048, 1408], P(('row', 'exp'), None, 'col')
- expert_up_grad: float32 [16, 2048, 1408], P(('row', 'exp'), None, 'col')
- expert_down_grad: float32 [16, 1408, 2048], P(('row', 'exp'), 'col')
Inputs may be any that keep to these rules, and one draw needn't show every extreme that they name: `routes`: each token names 6 different experts. Among the 512 tokens of one block at most 274 name the same expert, and that many do for some expert. `segments`: within each block the ids never fall; a document is one run of equal ids, of 128 to 384 tokens.
All inputs are finite; a program needn't handle non-finite values.
Results may differ from a plain program's by a relative error of at most 0.024.
Values may be sent and summed in bfloat16 or wider, within the bound.
No kernel may reach another device: no remote copies, remote signals or barrier semaphores. Data moves between devices by JAX's collectives and lax.ppermute only.
A program may use at most 384 MiB of HBM per device.

v0:
```python
import jax
import jax.numpy as jnp
from jax import lax
from jax.sharding import PartitionSpec as P

NOPE = 128
ROPE = 64
VDIM = 128
RANK = 512
TOP = 6


EPS = 1e-06
ROUTE_SCALE = 2.446
ROPE_BASE = 50000.0


def matmul(left, right):
    return jnp.dot(left, right, preferred_element_type=jnp.float32)


def rotary_tables(length, width):
    freqs = ROPE_BASE ** (
        -jnp.arange(width // 2, dtype=jnp.int32).astype(jnp.float32) * 2.0 / width
    )
    angles = jnp.arange(length, dtype=jnp.int32).astype(jnp.float32)[:, None] * freqs[None, :]
    return (jnp.cos(angles), jnp.sin(angles))


def rotary(values, cosine, sine):
    half = values.shape[-1] // 2
    first = values[..., :half]
    second = values[..., half:]
    return jnp.concatenate(
        [first * cosine - second * sine, second * cosine + first * sine], axis=-1
    )


def rotary_back(grads, cosine, sine):
    half = grads.shape[-1] // 2
    first = grads[..., :half]
    second = grads[..., half:]
    return jnp.concatenate(
        [first * cosine + second * sine, second * cosine - first * sine], axis=-1
    )


def swish_parts(values):
    sigma = 1.0 / (1.0 + jnp.exp(-values))
    return (values * sigma, sigma * (1.0 + values * (1.0 - sigma)))


def norm_back(grad_out, normed_hat, inverse, gain):
    scaled = gain * grad_out
    return inverse * (scaled - normed_hat * jnp.mean(scaled * normed_hat, axis=-1, keepdims=True))


def masked_scores(queries, keys_full, allowed):
    scores = jnp.einsum("thd,shd->hts", queries, keys_full, preferred_element_type=jnp.float32)
    return jnp.where(allowed[None], scores, -1e30)


def fill_slots(values, slot_index, count):
    return jnp.zeros((count + 1, values.shape[1]), values.dtype).at[slot_index].set(values)[:count]


def local(
    tokens,
    attn_gain,
    query_proj,
    latent_proj,
    latent_gain,
    keyval_proj,
    output_proj,
    mixer_gain,
    router_proj,
    shared_gate,
    shared_up,
    shared_down,
    expert_gate,
    expert_up,
    expert_down,
    routes,
    segments,
    cotangent,
):
    groups = lax.axis_size(("row", "exp"))
    columns = lax.axis_size("col")
    col_index = lax.axis_index("col")
    tok_rows, width = tokens.shape
    quarter = width // columns
    experts_all = expert_gate.shape[0] * groups
    capacity = 10 * tok_rows * TOP // (7 * experts_all)
    scale = (NOPE + ROPE) ** (-0.5)
    (
        gain_in,
        query_full,
        latent_full,
        gain_latent,
        keyval_full,
        output_full,
        gain_mid,
        router_full,
        shgate_full,
        shup_full,
        shdown_full,
    ) = (
        lax.all_gather(attn_gain, ("row", "exp"), axis=0, tiled=True),
        lax.all_gather(query_proj, ("row", "exp"), axis=0, tiled=True),
        lax.all_gather(latent_proj, ("row", "exp"), axis=0, tiled=True),
        lax.all_gather(latent_gain, ("row", "exp"), axis=0, tiled=True),
        lax.all_gather(keyval_proj, ("row", "exp"), axis=0, tiled=True),
        lax.all_gather(output_proj, ("row", "exp"), axis=1, tiled=True),
        lax.all_gather(mixer_gain, ("row", "exp"), axis=0, tiled=True),
        lax.all_gather(router_proj, ("row", "exp"), axis=0, tiled=True),
        lax.all_gather(shared_gate, ("row", "exp"), axis=0, tiled=True),
        lax.all_gather(shared_up, ("row", "exp"), axis=0, tiled=True),
        lax.all_gather(shared_down, ("row", "exp"), axis=1, tiled=True),
    )
    heads_dev = query_full.shape[1] // (NOPE + ROPE)
    cosine, sine = rotary_tables(tok_rows, ROPE)
    tokens_f = tokens.astype(jnp.float32)
    inverse_in = lax.rsqrt(jnp.mean(tokens_f * tokens_f, axis=-1, keepdims=True) + EPS)
    hat_in = tokens_f * inverse_in
    gainin_f = gain_in.astype(jnp.float32)
    normed_in = (hat_in * gainin_f).astype(jnp.bfloat16)
    query_raw = matmul(normed_in, query_full).reshape(tok_rows, heads_dev, NOPE + ROPE)
    queries = (
        jnp.concatenate(
            [query_raw[..., :NOPE], rotary(query_raw[..., NOPE:], cosine[:, None], sine[:, None])],
            axis=-1,
        )
        * scale
    ).astype(jnp.bfloat16)
    latent_part = matmul(normed_in, latent_full).astype(jnp.bfloat16)
    latent = lax.all_gather(latent_part, "col", axis=1, tiled=True).astype(jnp.float32)
    latent_rows = latent[:, :RANK]
    inverse_lat = lax.rsqrt(jnp.mean(latent_rows * latent_rows, axis=-1, keepdims=True) + EPS)
    hat_lat = latent_rows * inverse_lat
    gainlat_f = gain_latent.astype(jnp.float32)
    latent_norm = (hat_lat * gainlat_f).astype(jnp.bfloat16)
    key_rope = rotary(latent[:, RANK:], cosine, sine)
    keyval = matmul(latent_norm, keyval_full).reshape(tok_rows, heads_dev, NOPE + VDIM)
    keys_full = jnp.concatenate(
        [keyval[..., :NOPE], jnp.broadcast_to(key_rope[:, None, :], (tok_rows, heads_dev, ROPE))],
        axis=-1,
    ).astype(jnp.bfloat16)
    value_rows = keyval[..., NOPE:].astype(jnp.bfloat16)
    position = jnp.arange(tok_rows, dtype=jnp.int32)
    seg_ids = segments[0]
    allowed = (position[None, :] <= position[:, None]) & (seg_ids[:, None] == seg_ids[None, :])
    scores = masked_scores(queries, keys_full, allowed)
    biggest = jnp.max(scores, axis=-1, keepdims=True)
    expos = jnp.exp(scores - biggest)
    totals = jnp.sum(expos, axis=-1, keepdims=True)
    log_total = biggest + jnp.log(totals)
    probs_low = (expos / totals).astype(jnp.bfloat16)
    attended = (
        jnp.einsum("hts,shd->thd", probs_low, value_rows, preferred_element_type=jnp.float32)
        .astype(jnp.bfloat16)
        .reshape(tok_rows, heads_dev * VDIM)
    )
    attn_sum = lax.psum(matmul(attended, output_full), "col")
    hidden_sum = tokens_f + attn_sum
    inverse_mid = lax.rsqrt(jnp.mean(hidden_sum * hidden_sum, axis=-1, keepdims=True) + EPS)
    hat_mid = hidden_sum * inverse_mid
    gainmid_f = gain_mid.astype(jnp.float32)
    normed_mid = (hat_mid * gainmid_f).astype(jnp.bfloat16)
    logits = matmul(normed_mid, router_full)
    rexpos = jnp.exp(logits - jnp.max(logits, axis=-1, keepdims=True))
    router_prob = rexpos / jnp.sum(rexpos, axis=-1, keepdims=True)
    chosen = routes[:, :, None] == jnp.arange(experts_all, dtype=jnp.int32)[None, None, :]
    route_weight = ROUTE_SCALE * jnp.sum(jnp.where(chosen, router_prob[:, None, :], 0.0), axis=-1)
    shgate_val = matmul(normed_mid, shgate_full)
    shup_val = matmul(normed_mid, shup_full)
    shact, shslope = swish_parts(shgate_val)
    shared_hidden = (shact * shup_val).astype(jnp.bfloat16)
    shared_part = matmul(shared_hidden, shdown_full)
    flat_routes = routes.reshape(-1)
    hits = (flat_routes[:, None] == jnp.arange(experts_all, dtype=jnp.int32)[None, :]).astype(
        jnp.int32
    )
    slot_in = jnp.sum(hits * (jnp.cumsum(hits, axis=0) - 1), axis=1)
    owner_rows = jnp.arange(tok_rows * TOP, dtype=jnp.int32) // TOP
    live = slot_in >= 0
    slot_index = flat_routes * capacity + slot_in
    gate_w, up_weight, down_w = (expert_gate, expert_up, expert_down)
    slot_rows = experts_all * capacity
    live_f = live.astype(jnp.float32).reshape(tok_rows, TOP)[:, :, None]
    read_index = jnp.minimum(slot_index, slot_rows - 1)
    send_rows = fill_slots(normed_mid[owner_rows], slot_index, slot_rows)
    received_rows = lax.all_to_all(
        send_rows.reshape(experts_all, capacity, width),
        ("row", "exp"),
        split_axis=0,
        concat_axis=1,
        tiled=True,
    )
    egate_val = jnp.einsum(
        "bvn,bnl->bvl", received_rows, gate_w, preferred_element_type=jnp.float32
    )
    expert_up_value = jnp.einsum(
        "bvn,bnl->bvl", received_rows, up_weight, preferred_element_type=jnp.float32
    )
    expert_activation, expert_swish_slope = swish_parts(egate_val)
    expert_hidden_state = (expert_activation * expert_up_value).astype(jnp.bfloat16)
    expert_part = jnp.einsum(
        "esf,efd->esd", expert_hidden_state, down_w, preferred_element_type=jnp.float32
    )
    expert_own, shared_own = (
        lax.psum_scatter(expert_part, "col", scatter_dimension=2, tiled=True),
        lax.psum_scatter(shared_part, "col", scatter_dimension=1, tiled=True),
    )
    to_return = expert_own.astype(jnp.bfloat16)
    returned = lax.all_to_all(to_return, ("row", "exp"), split_axis=1, concat_axis=0, tiled=True)
    picked_rows = (
        returned.reshape(slot_rows, -1)[read_index].reshape(tok_rows, TOP, -1).astype(jnp.float32)
        * live_f
    )
    routed_part = jnp.sum(route_weight[:, :, None] * picked_rows, axis=1)
    hidden_own = lax.dynamic_slice_in_dim(hidden_sum, col_index * quarter, quarter, 1)
    cot_f = cotangent.astype(jnp.float32)
    cot_own = lax.dynamic_slice_in_dim(cot_f, col_index * quarter, quarter, 1)
    out_own = shared_own + routed_part
    weight_part = jnp.sum(cot_own[:, None, :] * picked_rows, axis=-1)
    layer_out = (hidden_own + out_own).astype(jnp.bfloat16)
    (
        gain_in,
        query_full,
        latent_full,
        gain_latent,
        keyval_full,
        output_full,
        gain_mid,
        router_full,
        shgate_full,
        shup_full,
        shdown_full,
    ) = (
        lax.all_gather(attn_gain, ("row", "exp"), axis=0, tiled=True),
        lax.all_gather(query_proj, ("row", "exp"), axis=0, tiled=True),
        lax.all_gather(latent_proj, ("row", "exp"), axis=0, tiled=True),
        lax.all_gather(latent_gain, ("row", "exp"), axis=0, tiled=True),
        lax.all_gather(keyval_proj, ("row", "exp"), axis=0, tiled=True),
        lax.all_gather(output_proj, ("row", "exp"), axis=1, tiled=True),
        lax.all_gather(mixer_gain, ("row", "exp"), axis=0, tiled=True),
        lax.all_gather(router_proj, ("row", "exp"), axis=0, tiled=True),
        lax.all_gather(shared_gate, ("row", "exp"), axis=0, tiled=True),
        lax.all_gather(shared_up, ("row", "exp"), axis=0, tiled=True),
        lax.all_gather(shared_down, ("row", "exp"), axis=1, tiled=True),
    )
    slot_grad = (route_weight.reshape(-1)[:, None] * cot_f[owner_rows]).astype(jnp.bfloat16)
    send_grads = fill_slots(slot_grad, slot_index, slot_rows)
    arrived_grad = lax.all_to_all(
        send_grads.reshape(experts_all, capacity, width),
        ("row", "exp"),
        split_axis=0,
        concat_axis=1,
        tiled=True,
    )
    expert_inner_gradient = jnp.einsum(
        "esd,efd->esf", arrived_grad, down_w, preferred_element_type=jnp.float32
    )
    expert_gate_gradient = (expert_inner_gradient * expert_up_value * expert_swish_slope).astype(
        jnp.bfloat16
    )
    expert_up_gradient = (expert_inner_gradient * expert_activation).astype(jnp.bfloat16)
    down_part = jnp.einsum(
        "esf,esd->efd", expert_hidden_state, arrived_grad, preferred_element_type=jnp.float32
    )
    gate_part = jnp.einsum(
        "pli,plm->pim", received_rows, expert_gate_gradient, preferred_element_type=jnp.float32
    )
    up_projection_piece = jnp.einsum(
        "pli,plm->pim", received_rows, expert_up_gradient, preferred_element_type=jnp.float32
    )
    rows_part = jnp.einsum(
        "wog,wcg->woc", expert_gate_gradient, gate_w, preferred_element_type=jnp.float32
    ) + jnp.einsum(
        "wog,wcg->woc", expert_up_gradient, up_weight, preferred_element_type=jnp.float32
    )
    shinner_grad = matmul(cotangent, shdown_full.T)
    shgate_grad = (shinner_grad * shup_val * shslope).astype(jnp.bfloat16)
    shup_grad = (shinner_grad * shact).astype(jnp.bfloat16)
    shdown_wgrad = matmul(shared_hidden.T, cotangent)
    shgate_wgrad = matmul(normed_mid.T, shgate_grad)
    shup_wgrad = matmul(normed_mid.T, shup_grad)
    shared_mid = matmul(shgate_grad, shgate_full.T) + matmul(shup_grad, shup_full.T)
    expert_gate_grad, expert_up_grad, expert_down_grad = (gate_part, up_projection_piece, down_part)
    rows_own, shared_mid_own = (
        lax.psum_scatter(rows_part, "col", scatter_dimension=2, tiled=True),
        lax.psum_scatter(shared_mid, "col", scatter_dimension=1, tiled=True),
    )
    to_back = rows_own.astype(jnp.bfloat16)
    rows_back = lax.all_to_all(to_back, ("row", "exp"), split_axis=1, concat_axis=0, tiled=True)
    routed_back = jnp.sum(
        rows_back.reshape(slot_rows, -1)[read_index].reshape(tok_rows, TOP, -1).astype(jnp.float32)
        * live_f,
        axis=1,
    )
    mid_own = shared_mid_own + routed_back
    mid_pieces, weight_pieces = (
        lax.all_gather(mid_own, "col", axis=1, tiled=True),
        lax.all_gather(weight_part, "col", axis=1, tiled=True),
    )
    weight_grad = jnp.sum(weight_pieces.reshape(tok_rows, columns, TOP), axis=1)
    prob_grad = ROUTE_SCALE * jnp.sum(jnp.where(chosen, weight_grad[:, :, None], 0.0), axis=1)
    logit_grad = (
        router_prob * (prob_grad - jnp.sum(router_prob * prob_grad, axis=-1, keepdims=True))
    ).astype(jnp.bfloat16)
    router_wgrad = matmul(normed_mid.T, logit_grad)
    mid_grad = mid_pieces + matmul(logit_grad, router_full.T)
    mixer_wgrad = jnp.sum(mid_grad * hat_mid, axis=0)
    hidden_grad = cot_f + norm_back(mid_grad, hat_mid, inverse_mid, gainmid_f)
    hidden_low = hidden_grad.astype(jnp.bfloat16)
    output_wgrad = matmul(attended.T, hidden_low)
    attended_grad = (
        matmul(hidden_low, output_full.T).astype(jnp.bfloat16).reshape(tok_rows, heads_dev, VDIM)
    )
    probs_again = jnp.exp(masked_scores(queries, keys_full, allowed) - log_total)
    prob_wgrad = jnp.einsum(
        "thd,shd->hts", attended_grad, value_rows, preferred_element_type=jnp.float32
    )
    score_grad = (
        probs_again * (prob_wgrad - jnp.sum(probs_again * prob_wgrad, axis=-1, keepdims=True))
    ).astype(jnp.bfloat16)
    value_grad = jnp.einsum(
        "hts,thd->shd",
        probs_again.astype(jnp.bfloat16),
        attended_grad,
        preferred_element_type=jnp.float32,
    )
    query_grad_full = (
        jnp.einsum("hts,shd->thd", score_grad, keys_full, preferred_element_type=jnp.float32)
        * scale
    )
    key_grad = jnp.einsum("hts,thd->shd", score_grad, queries, preferred_element_type=jnp.float32)
    query_raw_grad = jnp.concatenate(
        [
            query_grad_full[..., :NOPE],
            rotary_back(query_grad_full[..., NOPE:], cosine[:, None], sine[:, None]),
        ],
        axis=-1,
    )
    query_raw_grad = query_raw_grad.astype(jnp.bfloat16).reshape(
        tok_rows, heads_dev * (NOPE + ROPE)
    )
    query_wgrad = matmul(normed_in.T, query_raw_grad)
    keyval_rows_grad = (
        jnp.concatenate([key_grad[..., :NOPE], value_grad], axis=-1)
        .astype(jnp.bfloat16)
        .reshape(tok_rows, heads_dev * (NOPE + VDIM))
    )
    keyval_wgrad = matmul(latent_norm.T, keyval_rows_grad)
    latnorm_part = matmul(keyval_rows_grad, keyval_full.T)
    rope_part = jnp.sum(key_grad[..., NOPE:], axis=1)
    latnorm_grad, rope_grad = (
        lax.psum(latnorm_part.astype(jnp.bfloat16), "col").astype(jnp.float32),
        lax.psum(rope_part.astype(jnp.bfloat16), "col").astype(jnp.float32),
    )
    latgain_wgrad = jnp.sum(latnorm_grad * hat_lat, axis=0)
    latent_rows_grad = jnp.concatenate(
        [
            norm_back(latnorm_grad, hat_lat, inverse_lat, gainlat_f),
            rotary_back(rope_grad, cosine, sine),
        ],
        axis=-1,
    ).astype(jnp.bfloat16)
    latent_cols = latent_full.shape[1]
    latent_own_grad = lax.dynamic_slice_in_dim(
        latent_rows_grad, col_index * latent_cols, latent_cols, 1
    )
    latent_wgrad = matmul(normed_in.T, latent_own_grad)
    in_part = matmul(query_raw_grad, query_full.T) + matmul(latent_own_grad, latent_full.T)
    in_grad = lax.psum(in_part.astype(jnp.bfloat16), "col").astype(jnp.float32)
    gainin_wgrad = jnp.sum(in_grad * hat_in, axis=0)
    tokens_grad = hidden_grad + norm_back(in_grad, hat_in, inverse_in, gainin_f)
    (
        attn_gain_grad,
        query_grad,
        latent_grad,
        latent_gain_grad,
        keyval_grad,
        output_grad,
        mixer_gain_grad,
        router_grad,
        shared_gate_grad,
        shared_up_grad,
        shared_down_grad,
    ) = (
        lax.psum_scatter(
            gainin_wgrad.astype(jnp.bfloat16), ("row", "exp"), scatter_dimension=0, tiled=True
        ).astype(jnp.float32),
        lax.psum_scatter(
            query_wgrad.astype(jnp.bfloat16), ("row", "exp"), scatter_dimension=0, tiled=True
        ).astype(jnp.float32),
        lax.psum_scatter(
            latent_wgrad.astype(jnp.bfloat16), ("row", "exp"), scatter_dimension=0, tiled=True
        ).astype(jnp.float32),
        lax.psum_scatter(
            latgain_wgrad.astype(jnp.bfloat16), ("row", "exp"), scatter_dimension=0, tiled=True
        ).astype(jnp.float32),
        lax.psum_scatter(
            keyval_wgrad.astype(jnp.bfloat16), ("row", "exp"), scatter_dimension=0, tiled=True
        ).astype(jnp.float32),
        lax.psum_scatter(
            output_wgrad.astype(jnp.bfloat16), ("row", "exp"), scatter_dimension=1, tiled=True
        ).astype(jnp.float32),
        lax.psum_scatter(
            mixer_wgrad.astype(jnp.bfloat16), ("row", "exp"), scatter_dimension=0, tiled=True
        ).astype(jnp.float32),
        lax.psum_scatter(
            router_wgrad.astype(jnp.bfloat16), ("row", "exp"), scatter_dimension=0, tiled=True
        ).astype(jnp.float32),
        lax.psum_scatter(
            shgate_wgrad.astype(jnp.bfloat16), ("row", "exp"), scatter_dimension=0, tiled=True
        ).astype(jnp.float32),
        lax.psum_scatter(
            shup_wgrad.astype(jnp.bfloat16), ("row", "exp"), scatter_dimension=0, tiled=True
        ).astype(jnp.float32),
        lax.psum_scatter(
            shdown_wgrad.astype(jnp.bfloat16), ("row", "exp"), scatter_dimension=1, tiled=True
        ).astype(jnp.float32),
    )
    return (
        layer_out,
        tokens_grad,
        attn_gain_grad,
        query_grad,
        latent_grad,
        latent_gain_grad,
        keyval_grad,
        output_grad,
        mixer_gain_grad,
        router_grad,
        shared_gate_grad,
        shared_up_grad,
        shared_down_grad,
        expert_gate_grad,
        expert_up_grad,
        expert_down_grad,
    )


def solution(mesh):
    in_specs = (
        P(("row", "exp"), None),
        P(("row", "exp")),
        P(("row", "exp"), "col"),
        P(("row", "exp"), "col"),
        P(("row", "exp")),
        P(("row", "exp"), "col"),
        P("col", ("row", "exp")),
        P(("row", "exp")),
        P(("row", "exp"), None),
        P(("row", "exp"), "col"),
        P(("row", "exp"), "col"),
        P("col", ("row", "exp")),
        P(("row", "exp"), None, "col"),
        P(("row", "exp"), None, "col"),
        P(("row", "exp"), "col", None),
        P(("row", "exp"), None),
        P(("row", "exp"), None),
        P(("row", "exp"), None),
    )
    out_specs = (
        P(("row", "exp"), "col"),
        P(("row", "exp"), None),
        P(("row", "exp")),
        P(("row", "exp"), "col"),
        P(("row", "exp"), "col"),
        P(("row", "exp")),
        P(("row", "exp"), "col"),
        P("col", ("row", "exp")),
        P(("row", "exp")),
        P(("row", "exp"), None),
        P(("row", "exp"), "col"),
        P(("row", "exp"), "col"),
        P("col", ("row", "exp")),
        P(("row", "exp"), None, "col"),
        P(("row", "exp"), None, "col"),
        P(("row", "exp"), "col", None),
    )
    return jax.shard_map(local, mesh=mesh, in_specs=in_specs, out_specs=out_specs, check_vma=False)
```

profile of v0, /device:TPU:0, one launch (start us, length us, event | category | flops | bytes accessed | tf_op | source)
XLA Modules:
  0.0 2911.4 jit_solution(8041672926111857884)
XLA Ops:
  26.1 19.8 all_gather.51
  49.3 17.5 all_gather.52
  131.9 26.2 gather_fusion.2
  172.0 92.2 %all-reduce.10.cloned.1.call-done = f32[512,2048]{1,0:T(8,128)} async-done(((f32[512,2048]{1,0:T(8,128)}), f32[512,2048]{1,0:T(8,128)}) %all-reduce.10.cloned.1.call-update) | async-done | bytes 4194320 | tf_op jit(solution)/shard_map/psum | solution.py:163
  282.0 32.8 %scatter_custom_fusion.1 = bf16[4385,2048]{1,0:T(8,128)(2,1)} fusion(s32[3072]{0:T(1024)S(1)} %bitcast.150, f32[3072,2048]{1,0:T(8,128)} %mul.548, f32[3072,2048]{1,0:T(8,128)} %gather_fusion.2, bf16[]{:T(256)} %constant.67.clone.1), kind=kCustom, calls=%fused_computation.8 | custom fusion | flops 12582912 | bytes 68292608 | tf_op jit(solution)/shard_map/scatter | solution.py:64
  331.2 22.2 reshape.392
  359.4 25.7 gather_fusion
  385.1 28.7 scatter_custom_fusion
  430.2 22.4 reshape.390
  452.5 107.1 %all-to-all-done.2 = bf16[16,274,2048]{2,1,0:T(8,128)(2,1)} async-done(((bf16[16,274,2048]{2,1,0:T(8,128)(2,1)}), bf16[16,274,2048]{2,1,0:T(8,128)(2,1)}, u32[]{:S(2)}, u32[]{:S(2)}) %all-to-all-start.2) | async-done | bytes 17956896 | tf_op jit(solution)/shard_map/all_to_all | solution.py:254
  584.1 22.3 all_to_all.58
  606.5 194.0 %all-to-all-done = bf16[16,274,2048]{2,1,0:T(8,128)(2,1)} async-done(((bf16[16,274,2048]{2,1,0:T(8,128)(2,1)}), bf16[16,274,2048]{2,1,0:T(8,128)(2,1)}, u32[]{:S(2)}, u32[]{:S(2)}) %all-to-all-start) | async-done | bytes 17956896 | tf_op jit(solution)/shard_map/all_to_all | solution.py:192
  816.7 22.4 all_to_all.51
  865.8 21.6 multiply_convert_fusion.2
  887.4 19.1 fusion.90
  906.5 29.5 %convolution_add_fusion = f32[2,2192,2048]{2,1,0:T(8,128)} fusion(f32[2,2192,2048]{2,1,0:T(8,128)} %fusion.90, bf16[2,2192,352]{1,2,0:T(8,128)(2,1)} %get-tuple-element.32, bf16[2,2048,352]{1,2,0:T(8,128)(2,1)} %param.31), kind=kOutput, calls=%fused_computation.7 | convolution fusion | flops 6329794560 | bytes 77797376 | tf_op jit(solution)/shard_map/wog,wcg->woc/dot_general | solution.py:279
  936.0 18.9 fusion.88
  977.0 546.8 %reduce-scatter.19.cloned.1.call-done = f32[2,2192,512]{2,1,0:T(8,128)} async-done(((f32[2,2192,2048]{2,1,0:T(8,128)}), f32[2,2192,512]{2,1,0:T(8,128)}) %reduce-scatter.19.cloned.1.call-update) | async-done | bytes 8978448 | tf_op jit(solution)/shard_map/reduce_scatter | solution.py:291
  1527.9 20.4 copy.108
  1560.2 556.8 %reduce-scatter.15.cloned.1.call-done = f32[2,2192,512]{2,1,0:T(8,128)} async-done(((f32[2,2192,2048]{2,1,0:T(8,128)}), f32[2,2192,512]{2,1,0:T(8,128)}) %reduce-scatter.15.cloned.1.call-update) | async-done | bytes 8978448 | tf_op jit(solution)/shard_map/reduce_scatter | solution.py:211
  2121.1 20.6 copy.103
  2262.1 65.6 %all-gather.23.cloned.1.call-done = f32[512,2048]{1,0:T(8,128)} async-done(((f32[512,512]{1,0:T(8,128)}), f32[512,2048]{1,0:T(8,128)}) %all-gather.23.cloned.1.call-update) | async-done | bytes 4194320 | tf_op jit(solution)/shard_map/all_gather | solution.py:303
  2411.8 21.8 reduce-scatter.31.cloned.1.call-done
  2435.5 46.7 %reduce-scatter.33.cloned.1.call-done = bf16[256,704]{0,1:T(8,128)(2,1)} async-done(((bf16[2048,704]{0,1:T(8,128)(2,1)}), bf16[256,704]{0,1:T(8,128)(2,1)}) %reduce-scatter.33.cloned.1.call-update) | async-done | bytes 360464 | tf_op jit(solution)/shard_map/reduce_scatter | solution.py:418
  2484.0 46.7 %reduce-scatter.35.cloned.1.call-done = bf16[704,256]{1,0:T(8,128)(2,1)} async-done(((bf16[704,2048]{1,0:T(8,128)(2,1)}), bf16[704,256]{1,0:T(8,128)(2,1)}) %reduce-scatter.35.cloned.1.call-update) | async-done | bytes 360464 | tf_op jit(solution)/shard_map/reduce_scatter | solution.py:421
  2575.3 35.0 %reduce-scatter.13.cloned.1.call-done = f32[512,512]{1,0:T(8,128)} async-done(((f32[512,2048]{1,0:T(8,128)}), f32[512,512]{1,0:T(8,128)}) %reduce-scatter.13.cloned.1.call-update) | async-done | bytes 1048592 | tf_op jit(solution)/shard_map/reduce_scatter | solution.py:212
  2613.2 32.4 %reduce-scatter.29.cloned.1.call-done = bf16[256,16]{0,1:T(8,128)(2,1)} async-done(((bf16[2048,16]{0,1:T(8,128)(2,1)}), bf16[256,16]{0,1:T(8,128)(2,1)}) %reduce-scatter.29.cloned.1.call-update) | async-done | bytes 8208 | tf_op jit(solution)/shard_map/reduce_scatter | solution.py:412
  2646.9 35.1 %reduce-scatter.23.cloned.1.call-done = bf16[256,144]{0,1:T(8,128)(2,1)} async-done(((bf16[2048,144]{0,1:T(8,128)(2,1)}), bf16[256,144]{0,1:T(8,128)(2,1)}) %reduce-scatter.23.cloned.1.call-update) | async-done | bytes 73744 | tf_op jit(solution)/shard_map/reduce_scatter | solution.py:397
  2683.5 37.6 %reduce-scatter.25.cloned.1.call-done = bf16[64,1024]{1,0:T(8,128)(2,1)} async-done(((bf16[512,1024]{1,0:T(8,128)(2,1)}), bf16[64,1024]{1,0:T(8,128)(2,1)}) %reduce-scatter.25.cloned.1.call-update) | async-done | bytes 131088 | tf_op jit(solution)/shard_map/reduce_scatter | solution.py:403
  2722.8 86.8 %all-reduce.12.cloned.1.call-done = bf16[512,2048]{1,0:T(8,128)(2,1)} async-done(((bf16[512,2048]{1,0:T(8,128)(2,1)}), bf16[512,2048]{1,0:T(8,128)(2,1)}) %all-reduce.12.cloned.1.call-update) | async-done | bytes 2097168 | tf_op jit(solution)/shard_map/psum | solution.py:375
  2835.1 17.9 reduce-scatter.27.cloned.1.call-done
  2854.8 47.7 %reduce-scatter.21.cloned.1.call-done = bf16[256,768]{1,0:T(8,128)(2,1)} async-done(((bf16[2048,768]{1,0:T(8,128)(2,1)}), bf16[256,768]{1,0:T(8,128)(2,1)}) %reduce-scatter.21.cloned.1.call-update) | async-done | bytes 393232 | tf_op jit(solution)/shard_map/reduce_scatter | solution.py:394
  (378 shorter events, 553.7 us)
Async XLA Ops:
  7.2 858.6 %copy-start = (bf16[2,352,2048]{2,1,0:T(8,128)(2,1)S(1)}, bf16[2,352,2048]{2,1,0:T(8,128)(2,1)}, u32[]{:S(2)}) copy-start(bf16[2,352,2048]{2,1,0:T(8,128)(2,1)} %param.32) | copy-start | bytes 8650756
  7.2 78.8 %all-gather.11.cloned.1.call-start = ((), (), s32[]{:S(2)}) async-start(), calls=%async_computation.16 | async-start | bytes 1179648 | tf_op jit(solution)/shard_map/all_gather | solution.py:112
  7.9 85.6 %all-gather.13.cloned.1.call-start = ((), (), s32[]{:S(2)}) async-start(), calls=%async_computation.17 | async-start | bytes 3538944 | tf_op jit(solution)/shard_map/all_gather | solution.py:109
  8.7 95.3 %all-gather.15.cloned.1.call-start = ((), (), s32[]{:S(2)}) async-start(), calls=%async_computation.18 | async-start | bytes 2359296 | tf_op jit(solution)/shard_map/all_gather | solution.py:113
  9.4 254.8 %all-reduce.10.cloned.1.call-start = ((), (), s32[]{:S(2)}) async-start(), calls=%async_computation.19 | async-start | bytes 8388608 | tf_op jit(solution)/shard_map/psum | solution.py:163
  122.0 145.7 %copy-start.45 = (f32[8,1,256]{2,1,0:T(1,128)}, f32[8,1,256]{2,1,0:T(1,128)S(1)}, u32[]{:S(2)}) copy-start(f32[8,1,256]{2,1,0:T(1,128)S(1)} %convert_element_type.364) | copy-start | bytes 24580
  171.2 97.6 %copy-start.37 = (bf16[2048,16]{0,1:T(8,128)(2,1)}, bf16[2048,16]{0,1:T(8,128)(2,1)S(1)}, u32[]{:S(2)}) copy-start(bf16[2048,16]{0,1:T(8,128)(2,1)S(1)} %all_gather.61) | copy-start | bytes 196612
  171.4 96.3 %copy-start.51 = (s32[3072]{0:T(1024)}, s32[3072]{0:T(1024)S(1)}, u32[]{:S(2)}) copy-start(s32[3072]{0:T(1024)S(1)} %fusion.47) | copy-start | bytes 36868
  353.4 206.3 %all-to-all-start.2 = ((bf16[16,274,2048]{2,1,0:T(8,128)(2,1)}), bf16[16,274,2048]{2,1,0:T(8,128)(2,1)}, u32[]{:S(2)}, u32[]{:S(2)}) async-start(bf16[16,274,2048]{2,1,0:T(8,128)(2,1)} %reshape.392), calls=%async_computation.5 | async-start | bytes 36700160 | tf_op jit(solution)/shard_map/all_to_all | solution.py:254
  559.6 240.8 %all-to-all-start = ((bf16[16,274,2048]{2,1,0:T(8,128)(2,1)}), bf16[16,274,2048]{2,1,0:T(8,128)(2,1)}, u32[]{:S(2)}, u32[]{:S(2)}) async-start(bf16[16,274,2048]{2,1,0:T(8,128)(2,1)} %reshape.390), calls=%async_computation.1 | async-start | bytes 36700160 | tf_op jit(solution)/shard_map/all_to_all | solution.py:192
  565.5 389.5 %all-gather.17.cloned.1.call-start = ((), (), s32[]{:S(2)}) async-start(), calls=%async_computation.20 | async-start | bytes 3244032 | tf_op jit(solution)/shard_map/all_gather | solution.py:116
  566.1 394.2 %all-gather.19.cloned.1.call-start = ((), (), s32[]{:S(2)}) async-start(), calls=%async_computation.21 | async-start | bytes 3244032 | tf_op jit(solution)/shard_map/all_gather | solution.py:117
  566.6 399.0 %all-gather.21.cloned.1.call-start = ((), (), s32[]{:S(2)}) async-start(), calls=%async_computation.22 | async-start | bytes 3244032 | tf_op jit(solution)/shard_map/all_gather | solution.py:118
  567.4 956.4 %reduce-scatter.19.cloned.1.call-start = ((), (), s32[]{:S(2)}) async-start(), calls=%async_computation.26 | async-start | bytes 44892160 | tf_op jit(solution)/shard_map/reduce_scatter | solution.py:291
  936.0 1181.1 %reduce-scatter.15.cloned.1.call-start = ((), (), s32[]{:S(2)}) async-start(), calls=%async_computation.24 | async-start | bytes 44892160 | tf_op jit(solution)/shard_map/reduce_scatter | solution.py:211
  1548.3 593.4 %all-to-all-start.3 = ((bf16[2,2192,512]{2,0,1:T(2,128)(2,1)}), bf16[2,2192,512]{2,0,1:T(2,128)(2,1)}, u32[]{:S(2)}, u32[]{:S(2)}) async-start(bf16[2,2192,512]{2,0,1:T(2,128)(2,1)} %copy.108), calls=%async_computation.7 | async-start | bytes 8978432 | tf_op jit(solution)/shard_map/all_to_all | solution.py:295
  1552.9 691.4 %reduce-scatter.17.cloned.1.call-start = ((), (), s32[]{:S(2)}) async-start(), calls=%async_computation.25 | async-start | bytes 5242880 | tf_op jit(solution)/shard_map/reduce_scatter | solution.py:292
  2141.7 56.4 %all-to-all-start.1 = ((bf16[2,2192,512]{2,0,1:T(2,128)(2,1)}), bf16[2,2192,512]{2,0,1:T(2,128)(2,1)}, u32[]{:S(2)}, u32[]{:S(2)}) async-start(bf16[2,2192,512]{2,0,1:T(2,128)(2,1)} %copy.103), calls=%async_computation.3 | async-start | bytes 8978432 | tf_op jit(solution)/shard_map/all_to_all | solution.py:215
  2146.4 181.3 %all-gather.23.cloned.1.call-start = ((), (), s32[]{:S(2)}) async-start(), calls=%async_computation.27 | async-start | bytes 5242880 | tf_op jit(solution)/shard_map/all_gather | solution.py:303
  2247.1 138.1 %all-reduce.14.cloned.1.call-start = ((), (), s32[]{:S(2)}) async-start(), calls=%async_computation.37 | async-start | bytes 1179648 | tf_op jit(solution)/shard_map/psum | solution.py:358
  2347.2 86.4 %reduce-scatter.31.cloned.1.call-start = ((), (), s32[]{:S(2)}) async-start(), calls=%async_computation.34 | async-start | bytes 3244032 | tf_op jit(solution)/shard_map/reduce_scatter | solution.py:415
  2352.3 129.8 %reduce-scatter.33.cloned.1.call-start = ((), (), s32[]{:S(2)}) async-start(), calls=%async_computation.35 | async-start | bytes 3244032 | tf_op jit(solution)/shard_map/reduce_scatter | solution.py:418
  2357.4 173.3 %reduce-scatter.35.cloned.1.call-start = ((), (), s32[]{:S(2)}) async-start(), calls=%async_computation.36 | async-start | bytes 3244032 | tf_op jit(solution)/shard_map/reduce_scatter | solution.py:421
  2363.0 247.3 %reduce-scatter.13.cloned.1.call-start = ((), (), s32[]{:S(2)}) async-start(), calls=%async_computation.23 | async-start | bytes 5242880 | tf_op jit(solution)/shard_map/reduce_scatter | solution.py:212
  2369.0 276.6 %reduce-scatter.29.cloned.1.call-start = ((), (), s32[]{:S(2)}) async-start(), calls=%async_computation.33 | async-start | bytes 73728 | tf_op jit(solution)/shard_map/reduce_scatter | solution.py:412
  2371.7 310.2 %reduce-scatter.23.cloned.1.call-start = ((), (), s32[]{:S(2)}) async-start(), calls=%async_computation.30 | async-start | bytes 663552 | tf_op jit(solution)/shard_map/reduce_scatter | solution.py:397
  2394.5 326.6 %reduce-scatter.25.cloned.1.call-start = ((), (), s32[]{:S(2)}) async-start(), calls=%async_computation.31 | async-start | bytes 1179648 | tf_op jit(solution)/shard_map/reduce_scatter | solution.py:403
  2398.0 411.5 %all-reduce.12.cloned.1.call-start = ((), (), s32[]{:S(2)}) async-start(), calls=%async_computation.28 | async-start | bytes 4194304 | tf_op jit(solution)/shard_map/psum | solution.py:375
  2405.4 447.6 %reduce-scatter.27.cloned.1.call-start = ((), (), s32[]{:S(2)}) async-start(), calls=%async_computation.32 | async-start | bytes 2359296 | tf_op jit(solution)/shard_map/reduce_scatter | solution.py:406
  2410.3 492.2 %reduce-scatter.21.cloned.1.call-start = ((), (), s32[]{:S(2)}) async-start(), calls=%async_computation.29 | async-start | bytes 3538944 | tf_op jit(solution)/shard_map/reduce_scatter | solution.py:394
  2610.2 202.8 %copy-start.75 = (bf16[2048]{0:T(1024)(128)(2,1)S(1)}, bf16[2048]{0:T(1024)(128)(2,1)}, u32[]{:S(2)}) copy-start(bf16[2048]{0:T(1024)(128)(2,1)} %get-tuple-element.18) | copy-start | bytes 12292
  2610.2 202.8 %copy-start.80 = (bf16[512]{0:T(512)(128)(2,1)S(1)}, bf16[512]{0:T(512)(128)(2,1)}, u32[]{:S(2)}) copy-start(bf16[512]{0:T(512)(128)(2,1)} %get-tuple-element.22) | copy-start | bytes 3076
  (80 other events, 1152.8 us)
Sparse Core Ops, SparseCore 0:
  9.9 27.0 all-gather.10
  38.9 32.2 all-gather.12
  73.1 28.0 all-gather.14
  109.2 154.9 all-reduce.9
  567.8 46.6 all-gather.16
  616.2 104.2 all-gather.18
  722.4 79.2 all-gather.20
  936.1 587.6 reduce-scatter.18
  1526.2 590.7 reduce-scatter.14
  2119.7 77.5 reduce-scatter.16
  2247.3 80.4 all-gather.22
  2347.3 37.9 all-reduce.13
  2389.2 44.3 reduce-scatter.30
  2437.4 44.6 reduce-scatter.32
  2485.9 44.6 reduce-scatter.34
  2533.4 76.7 reduce-scatter.12
  2613.7 31.8 reduce-scatter.28
  2648.6 33.3 reduce-scatter.22
  2685.1 35.9 reduce-scatter.24
  2723.3 86.1 all-reduce.11
  2812.8 40.1 reduce-scatter.26
  2856.4 46.0 reduce-scatter.20
where the time goes:
time: 2920 us; the launch traced here: 2910 us
  waiting for transfers between devices  2000 us (68%)
  local copies, waits for them, and re-layouts  375 us (13%)
  matrix products  260 us (9%)
  blocking collectives  118 us (4%)
  other arithmetic  114 us (4%)
    reduce_scatter x1, waiting for transfers between devices, local(): lax.psum_scatter(expert_part, 'col', scatter_dimension=2, tiled=True)  557 us
    reduce_scatter x1, waiting for transfers between devices, local(): lax.psum_scatter(rows_part, 'col', scatter_dimension=2, tiled=True)  547 us
    all_to_all x1, waiting for transfers between devices, local(): lax.all_to_all(send_rows.reshape(experts_all, capacity, width), ('row', '...  194 us
    all_to_all x1, waiting for transfers between devices, local(): lax.all_to_all(send_grads.reshape(experts_all, capacity, width), ('row',...  107 us
    dot_general x24, matrix products, matmul(): return jnp.dot(left, right, preferred_element_type=jnp.float32)  96.1 us
    psum x1, waiting for transfers between devices, local(): attn_sum = lax.psum(matmul(attended, output_full), 'col')  92.2 us
    psum x1, waiting for transfers between devices, local(): in_grad = lax.psum(in_part.astype(jnp.bfloat16), 'col').astype(jnp.float32)  86.8 us
    all_gather x1, waiting for transfers between devices, local(): lax.all_gather(mid_own, 'col', axis=1, tiled=True)  65.6 us
  transfers between devices with their start and end apart: 26, of which 18 were waited for; matrix products, arithmetic and copies ran while one was open for 20% of the time, Pallas kernels for 0%

commit v1 on v0

v1 whole, which is shorter than its diff:
```python
import jax
import jax.numpy as jnp
from jax import lax
from jax.sharding import PartitionSpec as P

NOPE = 128
ROPE = 64
VDIM = 128
RANK = 512
TOP = 6
EPS = 1e-06
ROUTE_SCALE = 2.446
ROPE_BASE = 50000.0
BLOCKS = ("row", "exp")
LANES = 128
BF16 = jnp.bfloat16
F32 = jnp.float32


def matmul(left, right):
    return jnp.dot(left, right, preferred_element_type=F32)


def matmul_nt(left, right):
    return lax.dot_general(left, right, (((1,), (1,)), ((), ())), preferred_element_type=F32)


def matmul_tn(left, right):
    return lax.dot_general(left, right, (((0,), (0,)), ((), ())), preferred_element_type=F32)


def gather(values, axes, axis=0):
    return lax.all_gather(values, axes, axis=axis, tiled=True)


def scatter_sum(values, axes, axis=0):
    return lax.psum_scatter(values, axes, scatter_dimension=axis, tiled=True)


def rotary_tables(length, width):
    freqs = ROPE_BASE ** (
        -jnp.arange(width // 2, dtype=jnp.int32).astype(F32) * 2.0 / width
    )
    angles = jnp.arange(length, dtype=jnp.int32).astype(F32)[:, None] * freqs[None, :]
    return (jnp.cos(angles), jnp.sin(angles))


def rotary(values, cosine, sine):
    half = values.shape[-1] // 2
    first = values[..., :half]
    second = values[..., half:]
    return jnp.concatenate(
        [first * cosine - second * sine, second * cosine + first * sine], axis=-1
    )


def rotary_back(grads, cosine, sine):
    half = grads.shape[-1] // 2
    first = grads[..., :half]
    second = grads[..., half:]
    return jnp.concatenate(
        [first * cosine + second * sine, second * cosine - first * sine], axis=-1
    )


def swish_parts(values):
    sigma = 1.0 / (1.0 + jnp.exp(-values))
    return (values * sigma, sigma * (1.0 + values * (1.0 - sigma)))


def norm_back(grad_out, normed_hat, inverse, gain):
    scaled = gain * grad_out
    return inverse * (scaled - normed_hat * jnp.mean(scaled * normed_hat, axis=-1, keepdims=True))


def masked_scores(queries, keys_full, allowed):
    scores = jnp.einsum("thd,shd->hts", queries, keys_full, preferred_element_type=F32)
    return jnp.where(allowed[None], scores, -1e30)


def fill_slots(values, slot_index, count):
    return jnp.zeros((count + 1, values.shape[1]), values.dtype).at[slot_index].set(values)[:count]


def softmax_rows(logits):
    expos = jnp.exp(logits - jnp.max(logits, axis=-1, keepdims=True))
    return expos / jnp.sum(expos, axis=-1, keepdims=True)


def pad_rows(vector):
    rows = -(-vector.shape[0] // LANES)
    return jnp.pad(vector, (0, rows * LANES - vector.shape[0])).reshape(rows, LANES)


def pack_small(vectors):
    return jnp.concatenate([pad_rows(v.reshape(-1)) for v in vectors], axis=0)


def unpack_small(packed, groups, sizes):
    out, at = [], 0
    for size in sizes:
        rows = -(-size // LANES)
        piece = packed[:, at : at + rows].reshape(groups, rows * LANES)[:, :size]
        out.append(piece.reshape(-1))
        at += rows
    return out


def expert_columns(weights, wide):
    hidden = weights.shape[2]
    padded = jnp.pad(weights, ((0, 0), (0, 0), (0, wide - hidden)))
    return jnp.concatenate([padded[e] for e in range(weights.shape[0])], axis=1)


def dense_experts(rows_own, cot_all, member_all, router_full, expert_gate, expert_up, expert_down):
    owned, width, hidden = expert_gate.shape
    wide = -(-hidden // LANES) * LANES
    first = lax.axis_index(BLOCKS) * owned
    rows = gather(rows_own, BLOCKS)
    prob = softmax_rows(matmul(rows, router_full))
    weight = ROUTE_SCALE * jnp.where(member_all, prob, 0.0)
    weight = lax.dynamic_slice_in_dim(weight, first, owned, 1)
    member = lax.dynamic_slice_in_dim(member_all, first, owned, 1)
    spread = jnp.concatenate(
        [jnp.broadcast_to(weight[:, e : e + 1], (rows.shape[0], wide)) for e in range(owned)],
        axis=1,
    )
    gate_cols, up_cols = expert_columns(expert_gate, wide), expert_columns(expert_up, wide)
    down_rows = jnp.pad(expert_down, ((0, 0), (0, wide - hidden), (0, 0))).reshape(
        owned * wide, width
    )
    gate_val = matmul(rows, gate_cols)
    up_val = matmul(rows, up_cols)
    act, slope = swish_parts(gate_val)
    inner = (act * up_val).astype(BF16).astype(F32)
    inner_low = (inner * spread).astype(BF16)
    back = matmul_nt(cot_all, down_rows)
    products = jnp.sum((inner * back).reshape(-1, owned, wide), axis=-1)
    products = jnp.where(member, products, 0.0)
    inner_grad = back * spread
    both_grad = jnp.concatenate(
        [(inner_grad * up_val * slope).astype(BF16), (inner_grad * act).astype(BF16)], axis=1
    )
    out_part = matmul(inner_low, down_rows).astype(BF16)
    rows_part = matmul_nt(both_grad, jnp.concatenate([gate_cols, up_cols], axis=1)).astype(BF16)
    both_w = matmul_tn(rows, both_grad)
    down_w = matmul_tn(inner_low, cot_all)
    cut = lambda e, which: both_w[:, (which * owned + e) * wide :][:, :hidden]
    gate_w = jnp.stack([cut(e, 0) for e in range(owned)])
    up_w = jnp.stack([cut(e, 1) for e in range(owned)])
    down_w = down_w.reshape(owned, wide, width)[:, :hidden]
    return out_part, rows_part, products, first, (gate_w, up_w, down_w)


def routed_experts(rows_own, cot, routes, weight, expert_gate, expert_up, expert_down, capacity):
    tok_rows, width = rows_own.shape
    owned = expert_gate.shape[0]
    experts_all = owned * lax.axis_size(BLOCKS)
    flat_routes = routes.reshape(-1)
    hits = (flat_routes[:, None] == jnp.arange(experts_all, dtype=jnp.int32)[None, :]).astype(
        jnp.int32
    )
    slot_in = jnp.sum(hits * (jnp.cumsum(hits, axis=0) - 1), axis=1)
    owner_rows = jnp.arange(tok_rows * TOP, dtype=jnp.int32) // TOP
    slot_index = flat_routes * capacity + slot_in
    slot_rows = experts_all * capacity
    send = lambda v: lax.all_to_all(
        fill_slots(v, slot_index, slot_rows).reshape(experts_all, capacity, width),
        BLOCKS,
        split_axis=0,
        concat_axis=1,
        tiled=True,
    )
    receive = lambda v: lax.all_to_all(v, BLOCKS, split_axis=1, concat_axis=0, tiled=True).reshape(
        slot_rows, -1
    )[slot_index].reshape(tok_rows, TOP, -1).astype(F32)
    rows = send(rows_own[owner_rows])
    gate_val = jnp.einsum("bvn,bnl->bvl", rows, expert_gate, preferred_element_type=F32)
    up_val = jnp.einsum("bvn,bnl->bvl", rows, expert_up, preferred_element_type=F32)
    act, slope = swish_parts(gate_val)
    inner = (act * up_val).astype(BF16)
    out_part = jnp.einsum("esf,efd->esd", inner, expert_down, preferred_element_type=F32)
    picked = receive(scatter_sum(out_part, "col", 2).astype(BF16))
    routed_own = jnp.sum(weight[:, :, None] * picked, axis=1)
    quarter = routed_own.shape[1]
    cot_own = lax.dynamic_slice_in_dim(cot, lax.axis_index("col") * quarter, quarter, 1)
    weight_grad = lax.psum(jnp.sum(cot_own.astype(F32)[:, None, :] * picked, axis=-1), "col")
    slot_grad = (weight.reshape(-1)[:, None] * cot.astype(F32)[owner_rows]).astype(BF16)
    arrived = send(slot_grad)
    inner_grad = jnp.einsum("esd,efd->esf", arrived, expert_down, preferred_element_type=F32)
    gate_grad = (inner_grad * up_val * slope).astype(BF16)
    up_grad = (inner_grad * act).astype(BF16)
    down_w = jnp.einsum("esf,esd->efd", inner, arrived, preferred_element_type=F32)
    gate_w = jnp.einsum("pli,plm->pim", rows, gate_grad, preferred_element_type=F32)
    up_w = jnp.einsum("pli,plm->pim", rows, up_grad, preferred_element_type=F32)
    rows_part = jnp.einsum(
        "wog,wcg->woc", gate_grad, expert_gate, preferred_element_type=F32
    ) + jnp.einsum("wog,wcg->woc", up_grad, expert_up, preferred_element_type=F32)
    back_own = jnp.sum(receive(scatter_sum(rows_part, "col", 2).astype(BF16)), axis=1)
    to_rows = lambda v: lax.all_to_all(v, "col", split_axis=0, concat_axis=1, tiled=True)
    return to_rows(routed_own), to_rows(back_own), weight_grad, (gate_w, up_w, down_w)


def local(
    tokens,
    attn_gain,
    query_proj,
    latent_proj,
    latent_gain,
    keyval_proj,
    output_proj,
    mixer_gain,
    router_proj,
    shared_gate,
    shared_up,
    shared_down,
    expert_gate,
    expert_up,
    expert_down,
    routes,
    segments,
    cotangent,
):
    groups = lax.axis_size(BLOCKS)
    columns = lax.axis_size("col")
    col_index = lax.axis_index("col")
    tok_rows, width = tokens.shape
    own_rows = tok_rows // columns
    own = lambda v: lax.dynamic_slice_in_dim(v, col_index * own_rows, own_rows, 0)
    experts_all = expert_gate.shape[0] * groups
    capacity = 10 * tok_rows * TOP // (7 * experts_all)
    dense = groups * tok_rows <= 2 * expert_gate.shape[0] * groups * capacity
    scale = (NOPE + ROPE) ** (-0.5)
    query_cols, latent_cols = query_proj.shape[1], latent_proj.shape[1]
    sizes = [attn_gain.size, latent_gain.size, mixer_gain.size, router_proj.size]

    in_full = gather(jnp.concatenate([query_proj, latent_proj], axis=1), BLOCKS)
    small = gather(pack_small([attn_gain, latent_gain, mixer_gain, router_proj]), BLOCKS)
    gain_in, gain_latent, gain_mid, router_full = unpack_small(
        small.reshape(groups, -1, LANES), groups, sizes
    )
    gainin_f, gainlat_f, gainmid_f = (g.astype(F32) for g in (gain_in, gain_latent, gain_mid))
    router_full = router_full.reshape(width, experts_all)
    keyval_full = gather(keyval_proj, BLOCKS)
    output_t = gather(output_proj.T, BLOCKS)
    chosen = routes[:, :, None] == jnp.arange(experts_all, dtype=jnp.int32)[None, None, :]
    member = jnp.any(chosen, axis=1)
    shgate_full = gather(shared_gate, BLOCKS)
    shup_full = gather(shared_up, BLOCKS)
    shdown_t = gather(shared_down.T, BLOCKS)
    if dense:
        member_all = gather(member.astype(BF16), BLOCKS) > 0
        cot_all = gather(cotangent, BLOCKS)

    heads_dev = query_cols // (NOPE + ROPE)
    cosine, sine = rotary_tables(tok_rows, ROPE)
    tokens_f = tokens.astype(F32)
    inverse_in = lax.rsqrt(jnp.mean(tokens_f * tokens_f, axis=-1, keepdims=True) + EPS)
    hat_in = tokens_f * inverse_in
    normed_in = (hat_in * gainin_f).astype(BF16)
    in_out = matmul(normed_in, in_full)
    query_raw = in_out[:, :query_cols].reshape(tok_rows, heads_dev, NOPE + ROPE)
    queries = (
        jnp.concatenate(
            [query_raw[..., :NOPE], rotary(query_raw[..., NOPE:], cosine[:, None], sine[:, None])],
            axis=-1,
        )
        * scale
    ).astype(BF16)
    latent_part = in_out[:, query_cols:].astype(BF16)
    latent = gather(latent_part, "col", 1).astype(F32)
    latent_rows = latent[:, :RANK]
    inverse_lat = lax.rsqrt(jnp.mean(latent_rows * latent_rows, axis=-1, keepdims=True) + EPS)
    hat_lat = latent_rows * inverse_lat
    latent_norm = (hat_lat * gainlat_f).astype(BF16)
    key_rope = rotary(latent[:, RANK:], cosine, sine)
    keyval = matmul(latent_norm, keyval_full).reshape(tok_rows, heads_dev, NOPE + VDIM)
    keys_full = jnp.concatenate(
        [keyval[..., :NOPE], jnp.broadcast_to(key_rope[:, None, :], (tok_rows, heads_dev, ROPE))],
        axis=-1,
    ).astype(BF16)
    value_rows = keyval[..., NOPE:].astype(BF16)
    position = jnp.arange(tok_rows, dtype=jnp.int32)
    seg_ids = segments[0]
    allowed = (position[None, :] <= position[:, None]) & (seg_ids[:, None] == seg_ids[None, :])
    scores = masked_scores(queries, keys_full, allowed)
    biggest = jnp.max(scores, axis=-1, keepdims=True)
    expos = jnp.exp(scores - biggest)
    probs = expos / jnp.sum(expos, axis=-1, keepdims=True)
    probs_low = probs.astype(BF16)
    attended = (
        jnp.einsum("hts,shd->thd", probs_low, value_rows, preferred_element_type=F32)
        .astype(BF16)
        .reshape(tok_rows, heads_dev * VDIM)
    )
    attn_rows = scatter_sum(matmul_nt(attended, output_t).astype(BF16), "col")
    hidden_rows = own(tokens).astype(F32) + attn_rows.astype(F32)
    inverse_mid = lax.rsqrt(jnp.mean(hidden_rows * hidden_rows, axis=-1, keepdims=True) + EPS)
    hat_mid = hidden_rows * inverse_mid
    normed_rows = (hat_mid * gainmid_f).astype(BF16)
    normed_mid = gather(normed_rows, "col")

    shgate_val = matmul(normed_mid, shgate_full)
    shup_val = matmul(normed_mid, shup_full)
    shact, shslope = swish_parts(shgate_val)
    shared_hidden = (shact * shup_val).astype(BF16)
    shared_part = matmul_nt(shared_hidden, shdown_t)
    shinner_grad = matmul(cotangent, shdown_t)
    shgate_grad = (shinner_grad * shup_val * shslope).astype(BF16)
    shup_grad = (shinner_grad * shact).astype(BF16)
    shared_mid = matmul_nt(shgate_grad, shgate_full) + matmul_nt(shup_grad, shup_full)

    router_prob = softmax_rows(matmul(normed_rows, router_full))
    if dense:
        out_part, rows_part, products, first, expert_grads = dense_experts(
            normed_mid, cot_all, member_all, router_full, expert_gate, expert_up, expert_down
        )
        back_rows = scatter_sum(
            (scatter_sum(rows_part, BLOCKS).astype(F32) + shared_mid).astype(BF16), "col"
        ).astype(F32)
        placed = lax.dynamic_update_slice_in_dim(
            jnp.zeros((groups * tok_rows, experts_all), F32), products, first, 1
        )
        prob_grad = ROUTE_SCALE * scatter_sum(scatter_sum(placed, BLOCKS), "col")
        out_rows = scatter_sum(
            (scatter_sum(out_part, BLOCKS).astype(F32) + shared_part).astype(BF16), "col"
        ).astype(F32)
    else:
        probs_all = softmax_rows(matmul(normed_mid, router_full))
        weight = ROUTE_SCALE * jnp.sum(jnp.where(chosen, probs_all[:, None, :], 0.0), axis=-1)
        routed_rows, routed_back, weight_grad, expert_grads = routed_experts(
            normed_mid,
            cotangent,
            routes,
            weight,
            expert_gate,
            expert_up,
            expert_down,
            capacity,
        )
        out_rows = scatter_sum(shared_part.astype(BF16), "col").astype(F32) + routed_rows
        back_rows = scatter_sum(shared_mid.astype(BF16), "col").astype(F32) + routed_back
        prob_grad = own(
            ROUTE_SCALE * jnp.sum(jnp.where(chosen, weight_grad[:, :, None], 0.0), axis=1)
        )
    layer_rows = (hidden_rows + out_rows).astype(BF16)
    layer_out = lax.all_to_all(layer_rows, "col", split_axis=1, concat_axis=0, tiled=True)

    logit_grad = (
        router_prob * (prob_grad - jnp.sum(router_prob * prob_grad, axis=-1, keepdims=True))
    ).astype(BF16)
    router_wgrad = matmul_tn(normed_rows, logit_grad)
    mid_grad = back_rows + matmul_nt(logit_grad, router_full)
    mixer_wgrad = jnp.sum(mid_grad * hat_mid, axis=0)
    hidden_grad = own(cotangent).astype(F32) + norm_back(mid_grad, hat_mid, inverse_mid, gainmid_f)
    hidden_low = gather(hidden_grad.astype(BF16), "col")

    attended_grad = matmul(hidden_low, output_t).astype(BF16).reshape(tok_rows, heads_dev, VDIM)
    prob_wgrad = jnp.einsum(
        "thd,shd->hts", attended_grad, value_rows, preferred_element_type=F32
    )
    score_grad = (
        probs * (prob_wgrad - jnp.sum(probs * prob_wgrad, axis=-1, keepdims=True))
    ).astype(BF16)
    value_grad = jnp.einsum(
        "hts,thd->shd", probs_low, attended_grad, preferred_element_type=F32
    )
    query_grad_full = (
        jnp.einsum("hts,shd->thd", score_grad, keys_full, preferred_element_type=F32) * scale
    )
    key_grad = jnp.einsum("hts,thd->shd", score_grad, queries, preferred_element_type=F32)
    query_raw_grad = (
        jnp.concatenate(
            [
                query_grad_full[..., :NOPE],
                rotary_back(query_grad_full[..., NOPE:], cosine[:, None], sine[:, None]),
            ],
            axis=-1,
        )
        .astype(BF16)
        .reshape(tok_rows, query_cols)
    )
    keyval_rows_grad = (
        jnp.concatenate([key_grad[..., :NOPE], value_grad], axis=-1)
        .astype(BF16)
        .reshape(tok_rows, heads_dev * (NOPE + VDIM))
    )
    latnorm_part = matmul_nt(keyval_rows_grad, keyval_full)
    rope_part = jnp.sum(key_grad[..., NOPE:], axis=1)
    lat_sum = lax.psum(
        jnp.concatenate([latnorm_part, rope_part], axis=1).astype(BF16), "col"
    ).astype(F32)
    latnorm_grad, rope_grad = lat_sum[:, :RANK], lat_sum[:, RANK:]
    latgain_wgrad = jnp.sum(own(latnorm_grad * hat_lat), axis=0)
    latent_rows_grad = jnp.concatenate(
        [
            norm_back(latnorm_grad, hat_lat, inverse_lat, gainlat_f),
            rotary_back(rope_grad, cosine, sine),
        ],
        axis=-1,
    ).astype(BF16)
    latent_own_grad = lax.dynamic_slice_in_dim(
        latent_rows_grad, col_index * latent_cols, latent_cols, 1
    )
    in_cols_grad = jnp.concatenate([query_raw_grad, latent_own_grad], axis=1)
    in_rows = scatter_sum(matmul_nt(in_cols_grad, in_full).astype(BF16), "col").astype(F32)
    gainin_wgrad = jnp.sum(in_rows * own(hat_in), axis=0)
    token_rows = hidden_grad + norm_back(in_rows, own(hat_in), own(inverse_in), gainin_f)
    tokens_grad = gather(token_rows.astype(BF16), "col").astype(F32)

    reduce = lambda v: scatter_sum(v.astype(BF16), BLOCKS).astype(F32)
    shared_gate_grad = reduce(matmul_tn(normed_mid, shgate_grad))
    shared_up_grad = reduce(matmul_tn(normed_mid, shup_grad))
    shared_down_grad = reduce(matmul_tn(cotangent, shared_hidden)).T
    output_grad = reduce(matmul_tn(hidden_low, attended)).T
    keyval_grad = reduce(matmul_tn(latent_norm, keyval_rows_grad))
    in_wgrad = reduce(matmul_tn(normed_in, in_cols_grad))
    query_grad, latent_grad = in_wgrad[:, :query_cols], in_wgrad[:, query_cols:]
    pieces = [gainin_wgrad, latgain_wgrad, mixer_wgrad, router_wgrad.reshape(-1)]
    packed = jnp.stack(
        [
            pack_small([p.reshape(groups, -1)[g].astype(BF16) for p in pieces])
            for g in range(groups)
        ]
    )
    summed = lax.psum(lax.psum_scatter(packed, BLOCKS, scatter_dimension=0), "col").astype(F32)
    attn_gain_grad, latent_gain_grad, mixer_gain_grad, router_grad = unpack_small(
        summed[None], 1, sizes
    )
    return (
        layer_out,
        tokens_grad,
        attn_gain_grad,
        query_grad,
        latent_grad,
        latent_gain_grad,
        keyval_grad,
        output_grad,
        mixer_gain_grad,
        router_grad.reshape(router_proj.shape),
        shared_gate_grad,
        shared_up_grad,
        shared_down_grad,
        *expert_grads,
    )


def solution(mesh):
    rows, cols = P(BLOCKS, None), P(BLOCKS, "col")
    vector, turned = P(BLOCKS), P("col", BLOCKS)
    tall, flat = P(BLOCKS, None, "col"), P(BLOCKS, "col", None)
    in_specs = (
        rows, vector, cols, cols, vector, cols, turned, vector, rows, cols, cols, turned,
        tall, tall, flat, rows, rows, rows,
    )
    out_specs = (
        cols, rows, vector, cols, cols, vector, cols, turned, vector, rows, cols, cols, turned,
        tall, tall, flat,
    )
    return jax.shard_map(local, mesh=mesh, in_specs=in_specs, out_specs=out_specs, check_vma=False)
```

time: 2920 us -> 1400 us (0.48)
  waiting for transfers between devices: 2000 us -> 881 us
  local copies, waits for them, and re-layouts: 375 us -> 61.8 us
  other arithmetic: 114 us -> 53.7 us
  blocking collectives: 118 us -> 72.7 us
  matrix products: 260 us -> 304 us
    reduce_scatter x12 -> x14, waiting for transfers between devices: 1420 us -> 517 us  [scatter_sum(): return lax.psum_scatter(values, axes, scatter_dimension=axis, tiled=True)]
    all_to_all x4 -> x1, waiting for transfers between devices: 316 us -> 0.01 us  [local(): lax.all_to_all(layer_rows, 'col', split_axis=1, concat_axis=0, tiled=True)]
    all_gather x7 -> x11, waiting for transfers between devices: 65.7 us -> 298 us  [gather(): return lax.all_gather(values, axes, axis=axis, tiled=True)]
    psum x3 -> x1, waiting for transfers between devices: 192 us -> 35.2 us  [local(): lax.psum(jnp.concatenate([latnorm_part, rope_part], axis=1).astype(BF16),...]
    all_to_all x6 -> x1, local copies, waits for them, and re-layouts: 87.9 us -> 0.84 us  [local(): lax.all_to_all(layer_rows, 'col', split_axis=1, concat_axis=0, tiled=True)]
    gather x4 -> x0, local copies, waits for them, and re-layouts: 84.4 us -> none  [the longest x1 26.2 us: local(): cot_f[owner_rows]]
    reshape x5 -> x11, local copies, waits for them, and re-layouts: 55.2 us -> 1.33 us  [the longest x9 0.81 us: pad_rows(): jnp.pad(vector, (0, rows * LANES - vector.shape[0])).reshape(rows, LANES)]
    convert_element_type x5 -> x11, local copies, waits for them, and re-layouts: 54.6 us -> 0.96 us  [the longest x10 0.89 us: local(): p.reshape(groups, -1)[g].astype(BF16)]
  transfers between devices with their start and end apart: 26 -> 28, of which waited for: 18 -> 21; matrix products, arithmetic and copies ran while one was open for 20% -> 27% of each run, Pallas kernels for 0% -> 0%
where the time goes in v1:
time: 1400 us
  waiting for transfers between devices  881 us (63%)
  matrix products  304 us (22%)
  blocking collectives  72.7 us (5%)
  local copies, waits for them, and re-layouts  61.8 us (4%)
  other arithmetic  53.7 us (4%)
  between operations  16.2 us (1%)
    reduce_scatter x14, waiting for transfers between devices, scatter_sum(): return lax.psum_scatter(values, axes, scatter_dimension=axis, tiled=True)  517 us
    all_gather x11, waiting for transfers between devices, gather(): return lax.all_gather(values, axes, axis=axis, tiled=True)  298 us
    dot_general x11, matrix products, matmul(): return jnp.dot(left, right, preferred_element_type=F32)  133 us
    dot_general x9, matrix products, matmul_tn(): lax.dot_general(left, right, (((0,), (0,)), ((), ())), preferred_element_...  84.7 us
    dot_general x9, matrix products, matmul_nt(): lax.dot_general(left, right, (((1,), (1,)), ((), ())), preferred_element_...  79.9 us
    all_gather x3, blocking collectives, gather(): return lax.all_gather(values, axes, axis=axis, tiled=True)  53.3 us
    psum x1, waiting for transfers between devices, local(): lax.psum(jnp.concatenate([latnorm_part, rope_part], axis=1).astype(BF16),...  35.2 us
    unnamed x28, waiting for transfers between devices  30.6 us
  transfers between devices with their start and end apart: 28, of which 21 were waited for; matrix products, arithmetic and copies ran while one was open for 27% of the time, Pallas kernels for 0%

profile of v1, /device:TPU:0, one launch (start us, length us, event | category | flops | bytes accessed | tf_op | source)
XLA Modules:
  0.0 1395.8 jit_solution(11067067609486230640)
XLA Ops:
  14.1 18.2 %all-gather = bf16[8,37,128]{2,1,0:T(8,128)(2,1)S(1)} all-gather(bf16[1,37,128]{2,1,0:T(8,128)(2,1)S(1)} %maximum_bitcast_fusion), channel_id=1, replica_groups=mesh['row'=4,'col'=4,'exp'=2] {'row','exp'}, dimensions={0}, use_global_device_ids=true | all-gather | bytes 85248 | tf_op jit(solution)/shard_map/all_gather | solution.py:33
  34.8 15.3 %all-gather.13.cloned.1.call-done = bf16[2048,912]{1,0:T(8,128)(2,1)} async-done(((bf16[256,912]{1,0:T(8,128)(2,1)}), bf16[2048,912]{1,0:T(8,128)(2,1)}) %all-gather.13.cloned.1.call-update) | async-done | bytes 3735568 | tf_op jit(solution)/shard_map/all_gather | solution.py:33
  55.9 17.2 %all_gather.44 = bf16[512,576]{0,1:T(8,128)(2,1)S(1)} all-gather(bf16[512,144]{0,1:T(8,128)(2,1)S(1)} %slice.635), channel_id=1, replica_groups=mesh['row'=4,'col'=4,'exp'=2] {'col'}, dimensions={1}, use_global_device_ids=true | all-gather | bytes 737280 | tf_op jit(solution)/shard_map/all_gather | solution.py:33
  91.4 14.0 %all-gather.17.cloned.1.call-done = bf16[2048,512]{0,1:T(8,128)(2,1)} async-done(((bf16[256,512]{0,1:T(8,128)(2,1)}), bf16[2048,512]{0,1:T(8,128)(2,1)}) %all-gather.17.cloned.1.call-update) | async-done | bytes 2097168 | tf_op jit(solution)/shard_map/all_gather | solution.py:33
  109.7 43.7 %reduce-scatter.18.cloned.1.call-done = bf16[128,2048]{1,0:T(8,128)(2,1)} async-done(((bf16[512,2048]{1,0:T(8,128)(2,1)}), bf16[128,2048]{1,0:T(8,128)(2,1)}) %reduce-scatter.18.cloned.1.call-update) | async-done | bytes 524304 | tf_op jit(solution)/shard_map/reduce_scatter | solution.py:37
  157.9 44.4 %all-gather.19.cloned.1.call-done = bf16[512,2048]{1,0:T(8,128)(2,1)} async-done(((bf16[128,2048]{1,0:T(8,128)(2,1)}), bf16[512,2048]{1,0:T(8,128)(2,1)}) %all-gather.19.cloned.1.call-update) | async-done | bytes 2097168 | tf_op jit(solution)/shard_map/all_gather | solution.py:33
  204.9 17.9 %all_gather.49 = bf16[4096,16]{0,1:T(8,128)(2,1)S(1)} all-gather(bf16[512,16]{0,1:T(8,128)(2,1)S(1)} %convert_element_type.440), channel_id=1, replica_groups=mesh['row'=4,'col'=4,'exp'=2] {'row','exp'}, dimensions={0}, use_global_device_ids=true | all-gather | bytes 147456 | tf_op jit(solution)/shard_map/all_gather | solution.py:33
  229.3 63.7 %all-gather.29.cloned.1.call-done = bf16[4096,2048]{1,0:T(8,128)(2,1)} async-done(((bf16[512,2048]{1,0:T(8,128)(2,1)}), bf16[4096,2048]{1,0:T(8,128)(2,1)}) %all-gather.29.cloned.1.call-update) | async-done | bytes 16777232 | tf_op jit(solution)/shard_map/all_gather | solution.py:33
  293.1 20.3 %fusion.99 = f32[768,4096]{1,0:T(8,128)} fusion(bf16[768,2048]{1,0:T(8,128)(2,1)} %bitcast.215, bf16[4096,2048]{1,0:T(8,128)(2,1)} %all-gather.29.cloned.1.call-done), kind=kOutput, calls=%fused_computation.248 | convolution fusion | flops 12884901888 | bytes 32505856 | tf_op jit(solution)/shard_map/dot_general | solution.py:25
  313.4 71.3 %all-gather.21.cloned.1.call-done = bf16[4096,2048]{1,0:T(8,128)(2,1)} async-done(((bf16[512,2048]{1,0:T(8,128)(2,1)}), bf16[4096,2048]{1,0:T(8,128)(2,1)}) %all-gather.21.cloned.1.call-update) | async-done | bytes 16777232 | tf_op jit(solution)/shard_map/all_gather | solution.py:33
  384.7 10.4 fusion.95
  395.3 19.7 %fusion.23 = f32[4096,768]{0,1:T(8,128)} fusion(bf16[4096,2048]{1,0:T(8,128)(2,1)} %all-gather.21.cloned.1.call-done, bf16[2048,384]{0,1:T(8,128)(2,1)S(1)} %copy-done.36, bf16[2048,384]{0,1:T(8,128)(2,1)S(1)} %copy-done.37), kind=kOutput, calls=%fused_computation.44 | convolution fusion | flops 12891193344 | bytes 32505856 | tf_op jit(solution)/shard_map/dot_general | solution.py:21
  421.9 50.4 %multiply_convert_fusion.1 = (bf16[4096,768]{0,1:T(8,128)(2,1)}, bf16[4096,768]{0,1:T(8,128)(2,1)}, f32[4096,768]{0,1:T(8,128)}, bf16[4096,768]{0,1:T(8,128)(2,1)}) fusion(f32[4096,768]{0,1:T(8,128)} %fusion.23, f32[4096,384]{0,1:T(8,128)} %broadcast_in_dim.41, f32[4096,384]{0,1:T(8,128)} %broadcast_in_dim.39, f32[768,4096]{1,0:T(8,128)} %fusion.99, ...), kind=kOutput, calls=%fused_computation.10 | convolution fusion | flops 12950962176 | bytes 89128960 | tf_op jit(solution)/shard_map/dot_general | solution.py:21
  478.8 32.3 %convolution_convert_fusion = bf16[4096,2048]{1,0:T(8,128)(2,1)} fusion(bf16[4096,768]{0,1:T(8,128)(2,1)} %get-tuple-element.91, bf16[4096,768]{0,1:T(8,128)(2,1)} %get-tuple-element.90, bf16[2048,384]{0,1:T(8,128)(2,1)} %get-tuple-element.162, bf16[2048,384]{0,1:T(8,128)(2,1)} %get-tuple-element.163, bf16[2048,384]{0,1:T(8,128)(2,1)S(1)} %copy-done.35, ...), kind=kOutput, calls=%fused_computation.3 | convolution fusion | flops 25828524032 | bytes 35651584 | tf_op jit(solution)/shard_map/dot_general | solution.py:25
  513.0 23.3 %convolution_convert_fusion.1 = bf16[4096,2048]{1,0:T(8,128)(2,1)} fusion(bf16[768,2048]{1,0:T(8,128)(2,1)S(1)} %bitcast.216, bf16[4096,768]{0,1:T(8,128)(2,1)} %get-tuple-element.93, f32[4096,384]{0,1:T(8,128)} %broadcast_in_dim.41, f32[4096,384]{0,1:T(8,128)} %broadcast_in_dim.39), kind=kOutput, calls=%fused_computation.4 | convolution fusion | flops 12905873408 | bytes 38797312 | tf_op jit(solution)/shard_map/dot_general | solution.py:21
  559.8 82.1 %reduce-scatter.24.cloned.1.call-done = bf16[512,2048]{1,0:T(8,128)(2,1)} async-done(((bf16[4096,2048]{1,0:T(8,128)(2,1)}), bf16[512,2048]{1,0:T(8,128)(2,1)}) %reduce-scatter.24.cloned.1.call-update) | async-done | bytes 2097168 | tf_op jit(solution)/shard_map/reduce_scatter | solution.py:37
  648.3 113.4 %reduce-scatter.20.cloned.1.call-done = bf16[512,2048]{1,0:T(8,128)(2,1)} async-done(((bf16[4096,2048]{1,0:T(8,128)(2,1)}), bf16[512,2048]{1,0:T(8,128)(2,1)}) %reduce-scatter.20.cloned.1.call-update) | async-done | bytes 2097168 | tf_op jit(solution)/shard_map/reduce_scatter | solution.py:37
  769.2 13.8 reduce-scatter.30.cloned.1.call-done
  784.5 43.1 %reduce-scatter.26.cloned.1.call-done = bf16[128,2048]{1,0:T(8,128)(2,1)} async-done(((bf16[512,2048]{1,0:T(8,128)(2,1)}), bf16[128,2048]{1,0:T(8,128)(2,1)}) %reduce-scatter.26.cloned.1.call-update) | async-done | bytes 524304 | tf_op jit(solution)/shard_map/reduce_scatter | solution.py:37
  830.1 43.0 %reduce-scatter.22.cloned.1.call-done = bf16[128,2048]{1,0:T(8,128)(2,1)} async-done(((bf16[512,2048]{1,0:T(8,128)(2,1)}), bf16[128,2048]{1,0:T(8,128)(2,1)}) %reduce-scatter.22.cloned.1.call-update) | async-done | bytes 524304 | tf_op jit(solution)/shard_map/reduce_scatter | solution.py:37
  876.7 44.8 %all-gather.31.cloned.1.call-done = bf16[512,2048]{1,0:T(8,128)(2,1)} async-done(((bf16[128,2048]{1,0:T(8,128)(2,1)}), bf16[512,2048]{1,0:T(8,128)(2,1)}) %all-gather.31.cloned.1.call-update) | async-done | bytes 2097168 | tf_op jit(solution)/shard_map/all_gather | solution.py:33
  935.6 35.2 %all-reduce.14.cloned.1.call-done = bf16[512,576]{0,1:T(8,128)(2,1)} async-done(((bf16[512,576]{0,1:T(8,128)(2,1)}), bf16[512,576]{0,1:T(8,128)(2,1)}) %all-reduce.14.cloned.1.call-update) | async-done | bytes 589840 | tf_op jit(solution)/shard_map/psum | solution.py:390
  1007.1 14.3 %reduce-scatter.32.cloned.1.call-done = bf16[128,2048]{1,0:T(8,128)(2,1)} async-done(((bf16[512,2048]{1,0:T(8,128)(2,1)}), bf16[128,2048]{1,0:T(8,128)(2,1)}) %reduce-scatter.32.cloned.1.call-update) | async-done | bytes 524304 | tf_op jit(solution)/shard_map/reduce_scatter | solution.py:37
  1029.6 39.6 %reduce-scatter.44.cloned.1.call-done = bf16[256,704]{0,1:T(8,128)(2,1)} async-done(((bf16[2048,704]{0,1:T(8,128)(2,1)}), bf16[256,704]{0,1:T(8,128)(2,1)}) %reduce-scatter.44.cloned.1.call-update) | async-done | bytes 360464 | tf_op jit(solution)/shard_map/reduce_scatter | solution.py:37
  1071.1 46.8 %reduce-scatter.40.cloned.1.call-done = bf16[256,704]{0,1:T(8,128)(2,1)} async-done(((bf16[2048,704]{0,1:T(8,128)(2,1)}), bf16[256,704]{0,1:T(8,128)(2,1)}) %reduce-scatter.40.cloned.1.call-update) | async-done | bytes 360464 | tf_op jit(solution)/shard_map/reduce_scatter | solution.py:37
  1119.9 46.8 %reduce-scatter.42.cloned.1.call-done = bf16[256,704]{0,1:T(8,128)(2,1)} async-done(((bf16[2048,704]{0,1:T(8,128)(2,1)}), bf16[256,704]{0,1:T(8,128)(2,1)}) %reduce-scatter.42.cloned.1.call-update) | async-done | bytes 360464 | tf_op jit(solution)/shard_map/reduce_scatter | solution.py:37
  1168.6 35.3 %fusion.4 = f32[2048,1536]{0,1:T(8,128)} fusion(bf16[4096,2048]{1,0:T(8,128)(2,1)} %all-gather.21.cloned.1.call-done, bf16[4096,768]{0,1:T(8,128)(2,1)} %get-tuple-element.91, bf16[4096,768]{0,1:T(8,128)(2,1)} %get-tuple-element.90), kind=kOutput, calls=%fused_computation.14 | convolution fusion | flops 25794969600 | bytes 41943040 | tf_op jit(solution)/shard_map/dot_general | solution.py:29
  1206.3 22.1 %fusion.14 = f32[768,2048]{1,0:T(8,128)} fusion(bf16[4096,2048]{1,0:T(8,128)(2,1)} %all-gather.29.cloned.1.call-done, bf16[4096,768]{0,1:T(8,128)(2,1)} %get-tuple-element.93, f32[4096,384]{0,1:T(8,128)} %broadcast_in_dim.41, f32[4096,384]{0,1:T(8,128)} %broadcast_in_dim.39), kind=kOutput, calls=%fused_computation.36 | convolution fusion | flops 12897484800 | bytes 41943040 | tf_op jit(solution)/shard_map/dot_general | solution.py:29
  1257.9 26.4 %reduce-scatter.46.cloned.1.call-done = bf16[1,37,128]{2,1,0:T(8,128)(2,1)} async-done(((bf16[8,37,128]{2,1,0:T(8,128)(2,1)}), bf16[1,37,128]{2,1,0:T(8,128)(2,1)}) %reduce-scatter.46.cloned.1.call-update) | async-done | bytes 9488
  1284.3 19.3 %psum.15 = bf16[1,37,128]{2,1,0:T(8,128)(2,1)S(1)} all-reduce(bf16[1,37,128]{2,1,0:T(8,128)(2,1)} %reduce-scatter.46.cloned.1.call-done), channel_id=1, replica_groups=mesh['row'=4,'col'=4,'exp'=2] {'col'}, use_global_device_ids=true, to_apply=%region_30.31 | all-reduce | flops 4736 | bytes 18944 | tf_op jit(solution)/shard_map/psum | solution.py:426
  1305.5 30.4 %reduce-scatter.34.cloned.1.call-done = bf16[256,912]{0,1:T(8,128)(2,1)} async-done(((bf16[2048,912]{0,1:T(8,128)(2,1)}), bf16[256,912]{0,1:T(8,128)(2,1)}) %reduce-scatter.34.cloned.1.call-update) | async-done | bytes 466960 | tf_op jit(solution)/shard_map/reduce_scatter | solution.py:37
  1339.6 43.9 %all-gather.33.cloned.1.call-done = bf16[512,2048]{1,0:T(8,128)(2,1)} async-done(((bf16[128,2048]{1,0:T(8,128)(2,1)}), bf16[512,2048]{1,0:T(8,128)(2,1)}) %all-gather.33.cloned.1.call-update) | async-done | bytes 2097168 | tf_op jit(solution)/shard_map/all_gather | solution.py:33
  (378 shorter events, 216.9 us)
Async XLA Ops:
  7.2 42.9 %all-gather.13.cloned.1.call-start = ((), (), s32[]{:S(2)}) async-start(), calls=%async_computation.16 | async-start | bytes 4718592 | tf_op jit(solution)/shard_map/all_gather | solution.py:33
  10.3 65.1 %all-gather.15.cloned.1.call-start = ((), (), s32[]{:S(2)}) async-start(), calls=%async_computation.17 | async-start | bytes 1179648 | tf_op jit(solution)/shard_map/all_gather | solution.py:33
  11.0 94.4 %all-gather.17.cloned.1.call-start = ((), (), s32[]{:S(2)}) async-start(), calls=%async_computation.18 | async-start | bytes 2359296 | tf_op jit(solution)/shard_map/all_gather | solution.py:33
  11.7 141.7 %reduce-scatter.18.cloned.1.call-start = ((), (), s32[]{:S(2)}) async-start(), calls=%async_computation.19 | async-start | bytes 2621440 | tf_op jit(solution)/shard_map/reduce_scatter | solution.py:37
  109.6 92.7 %all-gather.19.cloned.1.call-start = ((), (), s32[]{:S(2)}) async-start(), calls=%async_computation.20 | async-start | bytes 2621440 | tf_op jit(solution)/shard_map/all_gather | solution.py:33
  157.3 65.6 %copy-start.21 = (bf16[2,2048,352]{1,2,0:T(8,128)(2,1)S(1)}, bf16[2,2048,352]{1,2,0:T(8,128)(2,1)}, u32[]{:S(2)}) copy-start(bf16[2,2048,352]{1,2,0:T(8,128)(2,1)} %param.30) | copy-start | bytes 8650756
  157.3 135.8 %all-gather.29.cloned.1.call-start = ((), (), s32[]{:S(2)}) async-start(), calls=%async_computation.27 | async-start | bytes 18874368 | tf_op jit(solution)/shard_map/all_gather | solution.py:33
  157.9 226.8 %all-gather.21.cloned.1.call-start = ((), (), s32[]{:S(2)}) async-start(), calls=%async_computation.21 | async-start | bytes 18874368 | tf_op jit(solution)/shard_map/all_gather | solution.py:33
  202.3 334.5 %all-gather.23.cloned.1.call-start = ((), (), s32[]{:S(2)}) async-start(), calls=%async_computation.23 | async-start | bytes 3244032 | tf_op jit(solution)/shard_map/all_gather | solution.py:33
  203.1 339.2 %all-gather.25.cloned.1.call-start = ((), (), s32[]{:S(2)}) async-start(), calls=%async_computation.24 | async-start | bytes 3244032 | tf_op jit(solution)/shard_map/all_gather | solution.py:33
  203.8 344.7 %all-gather.27.cloned.1.call-start = ((), (), s32[]{:S(2)}) async-start(), calls=%async_computation.25 | async-start | bytes 3244032 | tf_op jit(solution)/shard_map/all_gather | solution.py:33
  204.4 355.4 %reduce-scatter.28.cloned.1.call-start = ((), (), s32[]{:S(2)}) async-start(), calls=%async_computation.30 | async-start | bytes 294912 | tf_op jit(solution)/shard_map/reduce_scatter | solution.py:37
  204.9 179.9 %copy-start.12 = (bf16[2048,16]{1,0:T(8,128)(2,1)}, bf16[2048,16]{1,0:T(8,128)(2,1)S(1)}, u32[]{:S(2)}) copy-start(bf16[2048,16]{1,0:T(8,128)(2,1)S(1)} %reshape_reshape_reshape.6) | copy-start | bytes 196612
  313.4 81.9 %copy-start.36 = (bf16[2048,384]{0,1:T(8,128)(2,1)S(1)}, bf16[2048,384]{0,1:T(8,128)(2,1)}, u32[]{:S(2)}) copy-start(bf16[2048,384]{0,1:T(8,128)(2,1)} %get-tuple-element.162) | copy-start | bytes 4718596
  478.7 163.2 %reduce-scatter.24.cloned.1.call-start = ((), (), s32[]{:S(2)}) async-start(), calls=%async_computation.28 | async-start | bytes 18874368 | tf_op jit(solution)/shard_map/reduce_scatter | solution.py:37
  511.1 250.6 %reduce-scatter.20.cloned.1.call-start = ((), (), s32[]{:S(2)}) async-start(), calls=%async_computation.22 | async-start | bytes 18874368 | tf_op jit(solution)/shard_map/reduce_scatter | solution.py:37
  536.3 246.7 %reduce-scatter.30.cloned.1.call-start = ((), (), s32[]{:S(2)}) async-start(), calls=%async_computation.31 | async-start | bytes 40960 | tf_op jit(solution)/shard_map/reduce_scatter | solution.py:37
  555.9 86.1 %copy-start.71 = (bf16[2048,704]{0,1:T(8,128)(2,1)S(1)}, bf16[2048,704]{0,1:T(8,128)(2,1)}, u32[]{:S(2)}) copy-start(bf16[2048,704]{0,1:T(8,128)(2,1)} %all-gather.25.cloned.1.call-done) | copy-start | bytes 8650756
  559.8 267.8 %reduce-scatter.26.cloned.1.call-start = ((), (), s32[]{:S(2)}) async-start(), calls=%async_computation.29 | async-start | bytes 2621440 | tf_op jit(solution)/shard_map/reduce_scatter | solution.py:37
  648.3 224.9 %reduce-scatter.22.cloned.1.call-start = ((), (), s32[]{:S(2)}) async-start(), calls=%async_computation.26 | async-start | bytes 2621440 | tf_op jit(solution)/shard_map/reduce_scatter | solution.py:37
  767.6 153.8 %all-gather.31.cloned.1.call-start = ((), (), s32[]{:S(2)}) async-start(), calls=%async_computation.32 | async-start | bytes 2621440 | tf_op jit(solution)/shard_map/all_gather | solution.py:33
  876.5 94.3 %all-reduce.14.cloned.1.call-start = ((), (), s32[]{:S(2)}) async-start(), calls=%async_computation.33 | async-start | bytes 1179648 | tf_op jit(solution)/shard_map/psum | solution.py:390
  932.2 89.3 %reduce-scatter.32.cloned.1.call-start = ((), (), s32[]{:S(2)}) async-start(), calls=%async_computation.34 | async-start | bytes 2621440 | tf_op jit(solution)/shard_map/reduce_scatter | solution.py:37
  978.2 91.0 %reduce-scatter.44.cloned.1.call-start = ((), (), s32[]{:S(2)}) async-start(), calls=%async_computation.41 | async-start | bytes 3244032 | tf_op jit(solution)/shard_map/reduce_scatter | solution.py:37
  983.4 134.6 %reduce-scatter.40.cloned.1.call-start = ((), (), s32[]{:S(2)}) async-start(), calls=%async_computation.39 | async-start | bytes 3244032 | tf_op jit(solution)/shard_map/reduce_scatter | solution.py:37
  988.5 178.2 %reduce-scatter.42.cloned.1.call-start = ((), (), s32[]{:S(2)}) async-start(), calls=%async_computation.40 | async-start | bytes 3244032 | tf_op jit(solution)/shard_map/reduce_scatter | solution.py:37
  993.8 260.4 %reduce-scatter.36.cloned.1.call-start = ((), (), s32[]{:S(2)}) async-start(), calls=%async_computation.37 | async-start | bytes 1179648 | tf_op jit(solution)/shard_map/reduce_scatter | solution.py:37
  996.9 259.0 %reduce-scatter.38.cloned.1.call-start = ((), (), s32[]{:S(2)}) async-start(), calls=%async_computation.38 | async-start | bytes 2359296 | tf_op jit(solution)/shard_map/reduce_scatter | solution.py:37
  1002.5 281.8 %reduce-scatter.46.cloned.1.call-start = ((), (), s32[]{:S(2)}) async-start(), calls=%async_computation.42 | async-start | bytes 92160
  1024.0 311.9 %reduce-scatter.34.cloned.1.call-start = ((), (), s32[]{:S(2)}) async-start(), calls=%async_computation.36 | async-start | bytes 4202496 | tf_op jit(solution)/shard_map/reduce_scatter | solution.py:37
  1029.3 354.3 %all-gather.33.cloned.1.call-start = ((), (), s32[]{:S(2)}) async-start(), calls=%async_computation.35 | async-start | bytes 2621440 | tf_op jit(solution)/shard_map/all_gather | solution.py:33
  1229.3 25.0 %all-to-all-start = ((bf16[128,4,512]{2,0,1:T(8,128)(2,1)}), bf16[128,4,512]{2,0,1:T(8,128)(2,1)S(1)}, u32[]{:S(2)}, u32[]{:S(2)}) async-start(bf16[128,4,512]{2,0,1:T(8,128)(2,1)} %bitcast.207), calls=%async_computation.3 | async-start | bytes 1048576 | tf_op jit(solution)/shard_map/all_to_all | solution.py:347
  (72 other events, 1158.4 us)
Sparse Core Ops, SparseCore 0:
  10.5 39.5 all-gather.12
  52.0 23.3 all-gather.14
  77.3 28.0 all-gather.16
  109.7 43.6 reduce-scatter.17
  157.4 44.8 all-gather.18
  204.0 88.9 all-gather.28
  294.9 89.7 all-gather.20
  386.6 31.5 all-gather.22
  420.1 31.5 all-gather.24
  453.4 31.5 all-gather.26
  488.6 33.6 reduce-scatter.27
  525.7 116.1 reduce-scatter.23
  645.5 116.1 reduce-scatter.19
  763.8 19.2 reduce-scatter.29
  785.8 41.7 reduce-scatter.25
  830.3 42.8 reduce-scatter.21
  876.6 44.8 all-gather.30
  932.3 38.4 all-reduce.13
  978.3 43.0 reduce-scatter.31
  1025.3 43.9 reduce-scatter.43
  1073.2 44.7 reduce-scatter.39
  1121.9 44.6 reduce-scatter.41
  1169.8 35.9 reduce-scatter.35
  1209.0 41.1 reduce-scatter.37
  1253.7 30.5 reduce-scatter.45
  1287.7 48.1 reduce-scatter.33
  1337.9 45.6 all-gather.32
